TPU v7x, 256 devices: a whole 4x4x8 slice. The times are simulated.
256 devices in a mesh: seq: 32 (over z_lo, x, core), cam: 4 (over y), tp: 2 (over z_hi).
Axes of the slice: x: 4, y: 4, z: 8 (z_hi: 2, z_lo: 4; z = z_hi * 4 + z_lo), core: 2. Of those that a mesh axis runs over, the one named last changes fastest.
Arguments:
- pixel_feature: bfloat16 [32768, 2048], P(('seq', 'cam'), 'tp'), may hold values from -6 to 6
- depth_score: float32 [32768, 59], P(('seq', 'cam')), may hold values from 0.05 to 5
- depth_bin: int32 [32768, 4], P(('seq', 'cam')), may hold values from 0 to 58
- cell_owner: int32 [131072, 1], P(('seq', 'cam')), may hold values from 0 to 31; in each aligned block of 1024 rows (0 to 1023, 1024 to 2047, ...) at most 64 rows name the same one
- cell_local: int32 [32768, 4], P(('seq', 'cam')), may hold values from 0 to 7
- frame_keep: int32 [64], replicated, may hold values 0 or 1
- norm_gain: float32 [2048], P('tp'), may hold values from 0.1 to 1.9
- w_query: bfloat16 [2048, 2048], P(None, ('cam', 'tp')), may hold values from -1.5 to 1.5
- w_key: bfloat16 [2048, 2048], P(None, ('cam', 'tp')), may hold values from -0.375 to 0.375
- w_value: bfloat16 [2048, 2048], P(None, ('cam', 'tp')), may hold values from -0.125 to 0.125
Outputs:
- attended: bfloat16 [16384, 2048], P('seq', ('cam', 'tp'))
Inputs may be any that keep to these rules, and one draw needn't show every extreme that they name: `cell_owner`: among the 1024 points of one index of seq and cam (aligned blocks of rows), no owner is named more than 64 times, a bound that some block reaches.
All inputs are finite; a program needn't handle non-finite values.
Results may differ from a plain program's by a relative error of at most 0.028.
The roundings to bfloat16 on the way count: a program that leaves them out, or rounds other values in their place, can miss the bound.
Values may be sent and summed in bfloat16 or wider, within the bound.
A program may use at most 64 MiB of HBM per device.

v0:
```python
import jax
import jax.numpy as jnp
from jax import lax
from jax.sharding import PartitionSpec as P

D = 2048
HD = 128
CELL_DEV = 8
epsilon = 1e-05
block_rows = 512


def attend(state, query, query_start, keys, values, key_start, frame_keep):
    frames = frame_keep.shape[0]
    frame_query = (query_start + jnp.arange(query.shape[0], dtype=jnp.int32)) % frames
    frame_key = (key_start + jnp.arange(keys.shape[0], dtype=jnp.int32)) % frames
    frame_list = jnp.arange(frames, dtype=jnp.int32)
    kept = jnp.sum(
        jnp.where(frame_key[:, None] == frame_list[None, :], frame_keep[None, :], 0), axis=1
    )
    allowed = (frame_key[None, :] <= frame_query[:, None]) & (
        (kept[None, :] > 0) | (frame_key[None, :] == frame_query[:, None])
    )
    scores = jnp.einsum("qhd,khd->hqk", query, keys, preferred_element_type=jnp.float32) * (
        1.0 / HD**0.5
    )
    accum, peak, total = state
    new_peak = jnp.maximum(peak, jnp.max(jnp.where(allowed[None], scores, -1e30), axis=2))
    factor = jnp.exp(peak - new_peak)
    expo = jnp.where(allowed[None], jnp.exp(scores - new_peak[:, :, None]), 0.0)
    mixed = jnp.einsum(
        "hqk,khd->hqd", expo.astype(jnp.bfloat16), values, preferred_element_type=jnp.float32
    )
    return (accum * factor[:, :, None] + mixed, new_peak, total * factor + jnp.sum(expo, axis=2))


def local(
    pixel_feature,
    depth_score,
    depth_bin,
    cell_owner,
    cell_local,
    frame_keep,
    norm_gain,
    w_query,
    w_key,
    w_value,
):
    pixels, half = pixel_feature.shape
    keep_count = depth_bin.shape[1]
    points = pixels * keep_count
    seq_count = lax.axis_size("seq")
    seq_index = lax.axis_index("seq")
    frames = frame_keep.shape[0]
    frames_dev = frames // seq_count
    tokens_dev = CELL_DEV * frames
    capacity = 2 * points // seq_count
    prob = depth_score / jnp.sum(depth_score, axis=1, keepdims=True)
    bins = jnp.arange(depth_score.shape[1], dtype=jnp.int32)
    picked = jnp.sum(
        jnp.where(depth_bin[:, :, None] == bins[None, None, :], prob[:, None, :], 0.0), axis=2
    )
    weight = picked.astype(jnp.bfloat16)
    point_index = jnp.arange(points, dtype=jnp.int32).reshape(pixels, keep_count)
    local_frame = point_index // (points // frames_dev)
    owner = cell_owner[:, 0].reshape(pixels, keep_count)
    owner_flat = owner.reshape(points)
    hits = (owner_flat[:, None] == jnp.arange(seq_count, dtype=jnp.int32)[None, :]).astype(
        jnp.int32
    )
    rank = jnp.sum(jnp.cumsum(hits, axis=0) * hits, axis=1) - 1
    slot = owner_flat * capacity + rank
    point_rows = jnp.repeat(pixel_feature, keep_count, axis=0)
    send_rows = jnp.zeros((seq_count * capacity, half), jnp.bfloat16).at[slot].set(point_rows)
    send_rows = send_rows.reshape(seq_count, capacity, half)
    frame_global = seq_index * frames_dev + local_frame
    describe = jnp.stack(
        [
            weight.reshape(points),
            cell_local.reshape(points).astype(jnp.bfloat16),
            frame_global.reshape(points).astype(jnp.bfloat16),
        ],
        axis=0,
    )
    send_meta = jnp.zeros((3, seq_count * capacity), jnp.bfloat16).at[:, slot].set(describe)
    send_meta = send_meta.reshape(3, seq_count, capacity).transpose(1, 0, 2)
    got_rows, got_meta = (
        lax.all_to_all(send_rows, "seq", split_axis=0, concat_axis=0, tiled=True),
        lax.all_to_all(send_meta, "seq", split_axis=0, concat_axis=0, tiled=True),
    )
    target = (
        got_meta[:, 1, :].astype(jnp.float32) * frames + got_meta[:, 2, :].astype(jnp.float32)
    ).reshape(-1)
    token_ids = jnp.arange(tokens_dev, dtype=jnp.float32)
    mixing = jnp.where(
        token_ids[:, None] == target[None, :], got_meta[:, 0, :].reshape(-1)[None, :], 0
    )
    pooled = jnp.dot(mixing, got_rows.reshape(-1, half), preferred_element_type=jnp.float32)
    bev = lax.psum(pooled, "cam")
    squares = lax.psum(jnp.sum(bev * bev, axis=1), "tp")
    normed = (bev * lax.rsqrt(squares[:, None] / D + epsilon) * norm_gain[None, :]).astype(
        jnp.bfloat16
    )
    width = w_query.shape[1]
    heads_dev = width // HD
    piece = lax.all_gather(normed, "tp", axis=1, tiled=True)
    query_sum = jnp.dot(piece, w_query, preferred_element_type=jnp.float32)
    key_sum = jnp.dot(piece, w_key, preferred_element_type=jnp.float32)
    value_sum = jnp.dot(piece, w_value, preferred_element_type=jnp.float32)
    query = query_sum.astype(jnp.bfloat16).reshape(tokens_dev, heads_dev, HD)
    keys = key_sum.astype(jnp.bfloat16).reshape(tokens_dev, heads_dev, HD)
    values = value_sum.astype(jnp.bfloat16).reshape(tokens_dev, heads_dev, HD)
    query_start = seq_index * tokens_dev
    start_state = (
        jnp.zeros((heads_dev, tokens_dev, HD), jnp.float32),
        jnp.full((heads_dev, tokens_dev), -1e30, jnp.float32),
        jnp.zeros((heads_dev, tokens_dev), jnp.float32),
    )
    piece_keys = lax.all_gather(keys, "seq", axis=0, tiled=True)
    piece_values = lax.all_gather(values, "seq", axis=0, tiled=True)
    count = piece_keys.shape[0]

    def one_block(index, inner):
        block_keys = lax.dynamic_slice_in_dim(piece_keys, index * block_rows, block_rows, 0)
        block_values = lax.dynamic_slice_in_dim(piece_values, index * block_rows, block_rows, 0)
        return attend(
            inner, query, query_start, block_keys, block_values, index * block_rows, frame_keep
        )

    accum, peak, total = lax.fori_loop(0, count // block_rows, one_block, start_state)
    result = accum / total[:, :, None]
    return result.transpose(1, 0, 2).reshape(tokens_dev, width).astype(jnp.bfloat16)


def solution(mesh):
    return jax.shard_map(
        local,
        mesh=mesh,
        in_specs=(
            P(("seq", "cam"), "tp"),
            P(("seq", "cam"), None),
            P(("seq", "cam"), None),
            P(("seq", "cam"), None),
            P(("seq", "cam"), None),
            P(),
            P("tp"),
            P(None, ("cam", "tp")),
            P(None, ("cam", "tp")),
            P(None, ("cam", "tp")),
        ),
        out_specs=P("seq", ("cam", "tp")),
        check_vma=False,
    )
```

profile of v0, /device:TPU:1, one launch (start us, length us, event | category | flops | bytes accessed | tf_op | source)
XLA Modules:
  0.0 587.0 jit_solution(16973022452448787255)
XLA Ops:
  11.1 9.0 %reduce-window.6 = s32[32,8,128]{2,1,0:T(8,128)S(1)} reduce-window(s32[32,8,128]{2,1,0:T(8,128)S(1)} %fusion.34, s32[]{:T(128)} %constant.143.clone.1), window={size=1x1x128 pad=0_0x0_0x127_0}, to_apply=%region_0.0 | reduce-window | flops 4161536 | bytes 262148 | tf_op jit(solution)/shard_map/reduce-window
  22.4 3.3 scatter_custom_fusion
  26.7 10.0 %all-to-all-start = ((bf16[32,3,64]{2,1,0:T(4,128)(2,1)}), bf16[32,3,64]{2,1,0:T(4,128)(2,1)S(1)}, u32[]{:S(2)}, u32[]{:S(2)}) async-start(bf16[32,3,64]{2,1,0:T(4,128)(2,1)} %bitcast.8), calls=%async_computation | async-start | bytes 65536 | tf_op jit(solution)/shard_map/all_to_all | solution.py:89
  38.4 2.1 reshape.333
  40.4 8.6 %scatter_custom_fusion.1 = bf16[2048,1024]{1,0:T(8,128)(2,1)} fusion(s32[1024]{0:T(1024)S(1)} %bitcast.76, bf16[1024,1024]{1,0:T(8,128)(2,1)} %reshape.333, bf16[]{:T(256)} %constant.146.clone.1), kind=kCustom, calls=%fused_computation.44 | custom fusion | bytes 4194816 | tf_op jit(solution)/shard_map/scatter | solution.py:74
  49.0 7.8 %all-to-all-start.1 = ((bf16[32,64,1024]{2,1,0:T(8,128)(2,1)}), bf16[32,64,1024]{2,1,0:T(8,128)(2,1)}, u32[]{:S(2)}, u32[]{:S(2)}) async-start(bf16[32,64,1024]{2,1,0:T(8,128)(2,1)} %bitcast.65), calls=%async_computation.1 | async-start | bytes 8388608 | tf_op jit(solution)/shard_map/all_to_all | solution.py:88
  57.2 92.7 %all-to-all-done.1 = bf16[32,64,1024]{2,1,0:T(8,128)(2,1)} async-done(((bf16[32,64,1024]{2,1,0:T(8,128)(2,1)}), bf16[32,64,1024]{2,1,0:T(8,128)(2,1)}, u32[]{:S(2)}, u32[]{:S(2)}) %all-to-all-start.1) | async-done | bytes 4194336 | tf_op jit(solution)/shard_map/all_to_all | solution.py:88
  149.9 5.9 fusion.22
  155.8 64.2 %all-reduce.2.cloned.1.call-done = f32[512,1024]{1,0:T(8,128)} async-done(((f32[512,1024]{1,0:T(8,128)}), f32[512,1024]{1,0:T(8,128)}) %all-reduce.2.cloned.1.call-update) | async-done | bytes 2097168 | tf_op jit(solution)/shard_map/psum | solution.py:99
  221.9 7.8 %psum.15 = f32[512]{0:T(512)S(1)} all-reduce(f32[512]{0:T(512)S(1)} %multiply_reduce_fusion), channel_id=1, replica_groups=mesh['seq'=32,'cam'=4,'tp'=2] {'tp'}, use_global_device_ids=true, to_apply=%region_9.10 | all-reduce | flops 512 | bytes 4096 | tf_op jit(solution)/shard_map/psum | solution.py:100
  231.2 65.9 %all-gather.4.cloned.1.call-done = bf16[512,2048]{1,0:T(8,128)(2,1)} async-done(((bf16[512,1024]{1,0:T(8,128)(2,1)}), bf16[512,2048]{1,0:T(8,128)(2,1)}) %all-gather.4.cloned.1.call-update) | async-done | bytes 2097168 | tf_op jit(solution)/shard_map/all_gather | solution.py:106
  297.2 2.5 convolution_convert_fusion
  300.6 2.0 convolution_convert_fusion.2
  303.5 2.6 convolution_convert_fusion.1
  306.3 59.7 %all-gather.8.cloned.1.call-done = bf16[16384,2,128]{2,0,1:T(8,128)(2,1)} async-done(((bf16[512,2,128]{2,0,1:T(8,128)(2,1)}), bf16[16384,2,128]{2,0,1:T(8,128)(2,1)}) %all-gather.8.cloned.1.call-update) | async-done | bytes 8388624 | tf_op jit(solution)/shard_map/all_gather | solution.py:120
  366.0 69.0 %all-gather.6.cloned.1.call-done = bf16[16384,2,128]{2,0,1:T(8,128)(2,1)} async-done(((bf16[512,2,128]{2,0,1:T(8,128)(2,1)}), bf16[16384,2,128]{2,0,1:T(8,128)(2,1)}) %all-gather.6.cloned.1.call-update) | async-done | bytes 8388624 | tf_op jit(solution)/shard_map/all_gather | solution.py:119
  435.0 144.5 %while.20 = (s32[]{:T(128)}, f32[2,512,128]{2,1,0:T(8,128)S(1)}, f32[2,512]{1,0:T(2,128)S(1)}, f32[2,512]{1,0:T(2,128)S(1)}, s32[]{:T(128)}, /*index=5*/s32[64]{...) while((s32[]{:T(128)}, f32[2,512,128]{2,1,0:T(8,128)S(1)}, ...), condition=%wide.region_14.15_spmd.clone, body=%wide.region_10.14_spmd.clone.sunk | while | flops 275760128 | bytes 9256399 | solution.py:130
  437.5 2.0 convolution_add_fusion.2
  442.0 2.0 convolution_add_fusion.2
  446.5 2.0 convolution_add_fusion.2
  451.0 2.0 convolution_add_fusion.2
  455.5 2.0 convolution_add_fusion.2
  460.1 2.0 convolution_add_fusion.2
  464.6 2.0 convolution_add_fusion.2
  469.1 2.0 convolution_add_fusion.2
  473.6 2.0 convolution_add_fusion.2
  478.1 2.0 convolution_add_fusion.2
  482.7 2.0 convolution_add_fusion.2
  487.2 2.0 convolution_add_fusion.2
  491.7 2.0 convolution_add_fusion.2
  496.2 2.0 convolution_add_fusion.2
  500.7 2.0 convolution_add_fusion.2
  505.2 2.0 convolution_add_fusion.2
  509.8 2.0 convolution_add_fusion.2
  514.3 2.0 convolution_add_fusion.2
  518.8 2.0 convolution_add_fusion.2
  523.3 2.0 convolution_add_fusion.2
  527.8 2.0 convolution_add_fusion.2
  532.4 2.0 convolution_add_fusion.2
  536.9 2.0 convolution_add_fusion.2
  541.4 2.0 convolution_add_fusion.2
  545.9 2.0 convolution_add_fusion.2
  550.4 2.0 convolution_add_fusion.2
  554.9 2.0 convolution_add_fusion.2
  559.5 2.0 convolution_add_fusion.2
  564.0 2.0 convolution_add_fusion.2
  568.5 2.0 convolution_add_fusion.2
  573.0 2.0 convolution_add_fusion.2
  (347 shorter events, 97.8 us)
Async XLA Ops:
  6.5 290.6 %copy-start = (bf16[2048,256]{1,0:T(8,128)(2,1)S(1)}, bf16[2048,256]{1,0:T(8,128)(2,1)}, u32[]{:S(2)}) copy-start(bf16[2048,256]{1,0:T(8,128)(2,1)} %param.21) | copy-start | bytes 3145732
  26.7 22.4 %all-to-all-start = ((bf16[32,3,64]{2,1,0:T(4,128)(2,1)}), bf16[32,3,64]{2,1,0:T(4,128)(2,1)S(1)}, u32[]{:S(2)}, u32[]{:S(2)}) async-start(bf16[32,3,64]{2,1,0:T(4,128)(2,1)} %bitcast.8), calls=%async_computation | async-start | bytes 65536 | tf_op jit(solution)/shard_map/all_to_all | solution.py:89
  49.0 100.9 %all-to-all-start.1 = ((bf16[32,64,1024]{2,1,0:T(8,128)(2,1)}), bf16[32,64,1024]{2,1,0:T(8,128)(2,1)}, u32[]{:S(2)}, u32[]{:S(2)}) async-start(bf16[32,64,1024]{2,1,0:T(8,128)(2,1)} %bitcast.65), calls=%async_computation.1 | async-start | bytes 8388608 | tf_op jit(solution)/shard_map/all_to_all | solution.py:88
  56.8 163.2 %all-reduce.2.cloned.1.call-start = ((), (), s32[]{:S(2)}) async-start(), calls=%async_computation.2 | async-start | bytes 4194304 | tf_op jit(solution)/shard_map/psum | solution.py:99
  155.7 74.0 %copy-start.3 = (f32[1024]{0:T(1024)S(1)}, f32[1024]{0:T(1024)}, u32[]{:S(2)}) copy-start(f32[1024]{0:T(1024)} %param.18) | copy-start | bytes 12292
  155.8 141.4 %all-gather.4.cloned.1.call-start = ((), (), s32[]{:S(2)}) async-start(), calls=%async_computation.3 | async-start | bytes 3145728 | tf_op jit(solution)/shard_map/all_gather | solution.py:106
  220.0 9.7 %copy-start.1 = (f32[512,1024]{1,0:T(8,128)S(1)}, f32[512,1024]{1,0:T(8,128)}, u32[]{:S(2)}) copy-start(f32[512,1024]{1,0:T(8,128)} %all-reduce.2.cloned.1.call-done) | copy-start | bytes 6291460
  231.0 135.0 %all-gather.8.cloned.1.call-start = ((), (), s32[]{:S(2)}) async-start(), calls=%async_computation.5 | async-start | bytes 8650752 | tf_op jit(solution)/shard_map/all_gather | solution.py:120
  297.2 3.4 copy-start.4
  300.5 134.4 %all-gather.6.cloned.1.call-start = ((), (), s32[]{:S(2)}) async-start(), calls=%async_computation.4 | async-start | bytes 8650752 | tf_op jit(solution)/shard_map/all_gather | solution.py:119
  303.5 131.5 %copy-start.2 = (s32[64]{0:T(128)S(1)}, s32[64]{0:T(128)}, u32[]{:S(2)}) copy-start(s32[64]{0:T(128)} %param.17) | copy-start | bytes 772
Sparse Core Ops, SparseCore 0:
  155.9 64.0 all-reduce.1
  231.1 66.0 all-gather.3
  300.7 65.2 all-gather.7
  367.7 67.1 all-gather.5
where the time goes:
time: 590 us; the launch traced here: 587 us
  waiting for transfers between devices  352 us (60%)
  matrix products  124 us (21%)
  other arithmetic  50.4 us (9%)
  local copies, waits for them, and re-layouts  19.9 us (3%)
  starting transfers between devices  18.1 us (3%)
  between operations  13.3 us (2%)
  blocking collectives  7.76 us (1%)
    all_to_all x1, waiting for transfers between devices, local(): lax.all_to_all(send_rows, 'seq', split_axis=0, concat_axis=0, tiled=True)  92.7 us
    all_gather x1, waiting for transfers between devices, local(): piece_keys = lax.all_gather(keys, 'seq', axis=0, tiled=True)  69 us
    all_gather x1, waiting for transfers between devices, local(): piece = lax.all_gather(normed, 'tp', axis=1, tiled=True)  65.9 us
    psum x1, waiting for transfers between devices, local(): bev = lax.psum(pooled, 'cam')  64.2 us
    dot_general x32, matrix products, attend(): jnp.einsum('hqk,khd->hqd', expo.astype(jnp.bfloat16), values, preferred_e...  62.6 us
    all_gather x1, waiting for transfers between devices, local(): piece_values = lax.all_gather(values, 'seq', axis=0, tiled=True)  59.7 us
    dot_general x32, matrix products, attend(): jnp.einsum('qhd,khd->hqk', query, keys, preferred_element_type=jnp.float32)  48.2 us
    reduce_sum x32, other arithmetic, attend(): jnp.sum(expo, axis=2)  15.9 us
  transfers between devices with their start and end apart: 6, of which 5 were waited for; matrix products, arithmetic and copies ran while one was open for 3% of the time, Pallas kernels for 0%

commit v1 on v0

--- a/solution.py
+++ b/solution.py
@@ -96,7 +96,9 @@
         token_ids[:, None] == target[None, :], got_meta[:, 0, :].reshape(-1)[None, :], 0
     )
     pooled = jnp.dot(mixing, got_rows.reshape(-1, half), preferred_element_type=jnp.float32)
-    bev = lax.psum(pooled, "cam")
+    bev = pooled
+    for hop in (1, 2):
+        bev = bev + lax.ppermute(bev, "cam", [(dev, dev ^ hop) for dev in range(4)])
     squares = lax.psum(jnp.sum(bev * bev, axis=1), "tp")
     normed = (bev * lax.rsqrt(squares[:, None] / D + epsilon) * norm_gain[None, :]).astype(
         jnp.bfloat16

time: 590 us -> 619 us (1.049)
  waiting for transfers between devices: 352 us -> 379 us
    ppermute x0 -> x2, waiting for transfers between devices: none -> 88.9 us  [local(): bev = bev + lax.ppermute(bev, 'cam', [(dev, dev ^ hop) for dev in range(4)])]
    psum x1 -> x0, waiting for transfers between devices: 64.2 us -> none  [local(): bev = lax.psum(pooled, 'cam')]
  transfers between devices with their start and end apart: 6 -> 7, of which waited for: 5 -> 6; matrix products, arithmetic and copies ran while one was open for 3% -> 3% of each run, Pallas kernels for 0% -> 0%
where the time goes in v1:
time: 619 us; the launch traced here: 616 us
  waiting for transfers between devices  379 us (61%)
  matrix products  123 us (20%)
  other arithmetic  49.3 us (8%)
  starting transfers between devices  22.5 us (4%)
  local copies, waits for them, and re-layouts  19.9 us (3%)
  between operations  13.3 us (2%)
  blocking collectives  7.69 us (1%)
    all_to_all x1, waiting for transfers between devices, local(): lax.all_to_all(send_rows, 'seq', split_axis=0, concat_axis=0, tiled=True)  92.7 us
    ppermute x2, waiting for transfers between devices, local(): bev = bev + lax.ppermute(bev, 'cam', [(dev, dev ^ hop) for dev in range(4)])  88.9 us
    all_gather x1, waiting for transfers between devices, local(): piece_keys = lax.all_gather(keys, 'seq', axis=0, tiled=True)  69.1 us
    all_gather x1, waiting for transfers between devices, local(): piece = lax.all_gather(normed, 'tp', axis=1, tiled=True)  68.4 us
    dot_general x32, matrix products, attend(): jnp.einsum('hqk,khd->hqd', expo.astype(jnp.bfloat16), values, preferred_e...  62.6 us
    all_gather x1, waiting for transfers between devices, local(): piece_values = lax.all_gather(values, 'seq', axis=0, tiled=True)  59.7 us
    dot_general x32, matrix products, attend(): jnp.einsum('qhd,khd->hqk', query, keys, preferred_element_type=jnp.float32)  48.3 us
    reduce_sum x32, other arithmetic, attend(): jnp.sum(expo, axis=2)  15.9 us
  transfers between devices with their start and end apart: 7, of which 6 were waited for; matrix products, arithmetic and copies ran while one was open for 3% of the time, Pallas kernels for 0%

profile of v1, /device:TPU:1, one launch (start us, length us, event | category | flops | bytes accessed | tf_op | source)
XLA Modules:
  0.0 616.1 jit_solution(2584130061162451371)
XLA Ops:
  11.1 9.0 %reduce-window.6 = s32[32,8,128]{2,1,0:T(8,128)S(1)} reduce-window(s32[32,8,128]{2,1,0:T(8,128)S(1)} %fusion.34, s32[]{:T(128)} %constant.143.clone.1), window={size=1x1x128 pad=0_0x0_0x127_0}, to_apply=%region_0.0 | reduce-window | flops 4161536 | bytes 262148 | tf_op jit(solution)/shard_map/reduce-window
  22.4 3.3 scatter_custom_fusion
  26.7 10.0 %all-to-all-start = ((bf16[32,3,64]{2,1,0:T(4,128)(2,1)}), bf16[32,3,64]{2,1,0:T(4,128)(2,1)S(1)}, u32[]{:S(2)}, u32[]{:S(2)}) async-start(bf16[32,3,64]{2,1,0:T(4,128)(2,1)} %bitcast.8), calls=%async_computation | async-start | bytes 65536 | tf_op jit(solution)/shard_map/all_to_all | solution.py:89
  38.4 2.1 reshape.333
  40.4 8.6 %scatter_custom_fusion.1 = bf16[2048,1024]{1,0:T(8,128)(2,1)} fusion(s32[1024]{0:T(1024)S(1)} %bitcast.76, bf16[1024,1024]{1,0:T(8,128)(2,1)} %reshape.333, bf16[]{:T(256)} %constant.146.clone.1), kind=kCustom, calls=%fused_computation.44 | custom fusion | bytes 4194816 | tf_op jit(solution)/shard_map/scatter | solution.py:74
  49.0 7.8 %all-to-all-start.1 = ((bf16[32,64,1024]{2,1,0:T(8,128)(2,1)}), bf16[32,64,1024]{2,1,0:T(8,128)(2,1)}, u32[]{:S(2)}, u32[]{:S(2)}) async-start(bf16[32,64,1024]{2,1,0:T(8,128)(2,1)} %bitcast.65), calls=%async_computation.1 | async-start | bytes 8388608 | tf_op jit(solution)/shard_map/all_to_all | solution.py:88
  57.1 92.7 %all-to-all-done.1 = bf16[32,64,1024]{2,1,0:T(8,128)(2,1)} async-done(((bf16[32,64,1024]{2,1,0:T(8,128)(2,1)}), bf16[32,64,1024]{2,1,0:T(8,128)(2,1)}, u32[]{:S(2)}, u32[]{:S(2)}) %all-to-all-start.1) | async-done | bytes 4194336 | tf_op jit(solution)/shard_map/all_to_all | solution.py:88
  149.8 4.5 fusion.22
  155.9 44.9 %collective-permute-done = f32[512,1024]{1,0:T(8,128)S(1)} collective-permute-done((f32[512,1024]{1,0:T(8,128)S(1)}, f32[512,1024]{1,0:T(8,128)S(1)}, u32[]{:S(2)}, u32[]{:S(2)}) %collective-permute-start) | collective-permute-done | bytes 2097184 | tf_op jit(solution)/shard_map/ppermute | solution.py:101
  201.4 3.0 collective-permute-start.1
  204.4 44.0 %collective-permute-done.1 = f32[512,1024]{1,0:T(8,128)S(1)} collective-permute-done((f32[512,1024]{1,0:T(8,128)S(1)}, f32[512,1024]{1,0:T(8,128)S(1)}, u32[]{:S(2)}, u32[]{:S(2)}) %collective-permute-start.1) | collective-permute-done | bytes 2097184 | tf_op jit(solution)/shard_map/ppermute | solution.py:101
  248.7 7.7 %psum.7 = f32[512]{0:T(512)S(1)} all-reduce(f32[512]{0:T(512)S(1)} %get-tuple-element.315), channel_id=1, replica_groups=mesh['seq'=32,'cam'=4,'tp'=2] {'tp'}, use_global_device_ids=true, to_apply=%region_8.9 | all-reduce | flops 512 | bytes 4096 | tf_op jit(solution)/shard_map/psum | solution.py:102
  257.7 68.4 %all-gather.4.cloned.1.call-done = bf16[512,2048]{1,0:T(8,128)(2,1)} async-done(((bf16[512,1024]{1,0:T(8,128)(2,1)}), bf16[512,2048]{1,0:T(8,128)(2,1)}) %all-gather.4.cloned.1.call-update) | async-done | bytes 2097168 | tf_op jit(solution)/shard_map/all_gather | solution.py:108
  326.1 2.5 convolution_convert_fusion
  329.5 2.0 convolution_convert_fusion.2
  332.4 2.6 convolution_convert_fusion.1
  335.2 59.7 %all-gather.8.cloned.1.call-done = bf16[16384,2,128]{2,0,1:T(8,128)(2,1)} async-done(((bf16[512,2,128]{2,0,1:T(8,128)(2,1)}), bf16[16384,2,128]{2,0,1:T(8,128)(2,1)}) %all-gather.8.cloned.1.call-update) | async-done | bytes 8388624 | tf_op jit(solution)/shard_map/all_gather | solution.py:122
  394.9 69.1 %all-gather.6.cloned.1.call-done = bf16[16384,2,128]{2,0,1:T(8,128)(2,1)} async-done(((bf16[512,2,128]{2,0,1:T(8,128)(2,1)}), bf16[16384,2,128]{2,0,1:T(8,128)(2,1)}) %all-gather.6.cloned.1.call-update) | async-done | bytes 8388624 | tf_op jit(solution)/shard_map/all_gather | solution.py:121
  464.0 144.7 %while.20 = (s32[]{:T(128)}, f32[2,512,128]{2,1,0:T(8,128)S(1)}, f32[2,512]{1,0:T(2,128)S(1)}, f32[2,512]{1,0:T(2,128)S(1)}, s32[]{:T(128)}, /*index=5*/s32[64]{...) while((s32[]{:T(128)}, f32[2,512,128]{2,1,0:T(8,128)S(1)}, ...), condition=%wide.region_13.14_spmd.clone, body=%wide.region_9.13_spmd.clone.sunk | while | flops 275760128 | bytes 9256399 | solution.py:132
  466.5 2.0 convolution_add_fusion.2
  471.1 2.0 convolution_add_fusion.2
  475.6 2.0 convolution_add_fusion.2
  480.1 2.0 convolution_add_fusion.2
  484.6 2.0 convolution_add_fusion.2
  489.1 2.0 convolution_add_fusion.2
  493.7 2.0 convolution_add_fusion.2
  498.2 2.0 convolution_add_fusion.2
  502.7 2.0 convolution_add_fusion.2
  507.2 2.0 convolution_add_fusion.2
  511.8 2.0 convolution_add_fusion.2
  516.3 2.0 convolution_add_fusion.2
  520.8 2.0 convolution_add_fusion.2
  525.3 2.0 convolution_add_fusion.2
  529.8 2.0 convolution_add_fusion.2
  534.4 2.0 convolution_add_fusion.2
  538.9 2.0 convolution_add_fusion.2
  543.4 2.0 convolution_add_fusion.2
  547.9 2.0 convolution_add_fusion.2
  552.5 2.0 convolution_add_fusion.2
  557.0 2.0 convolution_add_fusion.2
  561.5 2.0 convolution_add_fusion.2
  566.0 2.0 convolution_add_fusion.2
  570.5 2.0 convolution_add_fusion.2
  575.1 2.0 convolution_add_fusion.2
  579.6 2.0 convolution_add_fusion.2
  588.6 2.0 convolution_add_fusion.2
  593.2 2.0 convolution_add_fusion.2
  606.7 2.0 convolution_add_fusion.2
  (347 shorter events, 102.1 us)
Async XLA Ops:
  6.5 319.5 %copy-start = (bf16[2048,256]{1,0:T(8,128)(2,1)S(1)}, bf16[2048,256]{1,0:T(8,128)(2,1)}, u32[]{:S(2)}) copy-start(bf16[2048,256]{1,0:T(8,128)(2,1)} %param.21) | copy-start | bytes 3145732
  26.7 22.3 %all-to-all-start = ((bf16[32,3,64]{2,1,0:T(4,128)(2,1)}), bf16[32,3,64]{2,1,0:T(4,128)(2,1)S(1)}, u32[]{:S(2)}, u32[]{:S(2)}) async-start(bf16[32,3,64]{2,1,0:T(4,128)(2,1)} %bitcast.8), calls=%async_computation | async-start | bytes 65536 | tf_op jit(solution)/shard_map/all_to_all | solution.py:89
  49.0 100.9 %all-to-all-start.1 = ((bf16[32,64,1024]{2,1,0:T(8,128)(2,1)}), bf16[32,64,1024]{2,1,0:T(8,128)(2,1)}, u32[]{:S(2)}, u32[]{:S(2)}) async-start(bf16[32,64,1024]{2,1,0:T(8,128)(2,1)} %bitcast.65), calls=%async_computation.1 | async-start | bytes 8388608 | tf_op jit(solution)/shard_map/all_to_all | solution.py:88
  56.8 269.3 %all-gather.4.cloned.1.call-start = ((), (), s32[]{:S(2)}) async-start(), calls=%async_computation.2 | async-start | bytes 3145728 | tf_op jit(solution)/shard_map/all_gather | solution.py:108
  154.4 46.5 %collective-permute-start = (f32[512,1024]{1,0:T(8,128)S(1)}, f32[512,1024]{1,0:T(8,128)S(1)}, u32[]{:S(2)}, u32[]{:S(2)}) collective-permute-start(f32[512,1024]{1,0:T(8,128)S(1)} %fusion.22), channel_id=1, source_target_pairs={{0,2},{2,0},{4,6},{6,4},{1,3},{3,1},{5,7},{7,5},{8,10},{10,8},{12,... | collective-permute-start | bytes 6291464 | tf_op jit(solution)/shard_map/ppermute | solution.py:101
  201.4 55.0 %copy-start.2 = (f32[1024]{0:T(1024)S(1)}, f32[1024]{0:T(1024)}, u32[]{:S(2)}) copy-start(f32[1024]{0:T(1024)} %param.18) | copy-start | bytes 12292
  201.4 47.0 %collective-permute-start.1 = (f32[512,1024]{1,0:T(8,128)S(1)}, f32[512,1024]{1,0:T(8,128)S(1)}, u32[]{:S(2)}, u32[]{:S(2)}) collective-permute-start(f32[512,1024]{1,0:T(8,128)S(1)} %add.221), channel_id=1, source_target_pairs={{0,4},{2,6},{4,0},{6,2},{1,5},{3,7},{5,1},{7,3},{8,12},{10,14},{12... | collective-permute-start | bytes 6291464 | tf_op jit(solution)/shard_map/ppermute | solution.py:101
  257.6 137.3 %all-gather.8.cloned.1.call-start = ((), (), s32[]{:S(2)}) async-start(), calls=%async_computation.4 | async-start | bytes 8650752 | tf_op jit(solution)/shard_map/all_gather | solution.py:122
  326.1 3.4 copy-start.3
  329.4 134.6 %all-gather.6.cloned.1.call-start = ((), (), s32[]{:S(2)}) async-start(), calls=%async_computation.3 | async-start | bytes 8650752 | tf_op jit(solution)/shard_map/all_gather | solution.py:121
  332.4 131.6 %copy-start.1 = (s32[64]{0:T(128)S(1)}, s32[64]{0:T(128)}, u32[]{:S(2)}) copy-start(s32[64]{0:T(128)} %param.17) | copy-start | bytes 772
Sparse Core Ops, SparseCore 0:
  257.8 68.2 all-gather.3
  329.6 65.2 all-gather.7
  396.8 67.1 all-gather.5
